TPU v7x, 512 devices: a whole 4x4x16 slice. The times are simulated.
512 devices in a mesh: seq: 32 (over x, y, core), head: 16 (over z).
Axes of the slice: x: 4, y: 4, z: 16, core: 2. Of those that a mesh axis runs over, the one named last changes fastest.
Arguments:
- queries: bfloat16 [32768, 4096], P('seq', 'head'), may hold values from -6 to 6
- keys: bfloat16 [32768, 4096], P('seq', 'head'), may hold values from -6 to 6
- values: bfloat16 [32768, 4096], P('seq', 'head'), may hold values from -6 to 6
- out_weight: bfloat16 [4096, 4096], P(None, 'head'), may hold values from -0.09375 to 0.09375
Outputs:
- output: bfloat16 [32768, 4096], P('seq', 'head')
All inputs are finite; a program needn't handle non-finite values.
Results may differ from a plain program's by a relative error of at most 0.0058.
Values may be sent and summed in bfloat16 or wider, within the bound.
A program may use at most 64 MiB of HBM per device.

v0:
```python
import jax
import jax.numpy as jnp
from jax import lax
from jax.sharding import PartitionSpec as P

HD = 128
BLOCK = 1024


def prefix_2(value, axis, join, neutral):
    count, mine = (lax.axis_size(axis), lax.axis_index(axis))
    pieces = lax.all_gather(value, axis)
    running = jnp.full_like(value, 0) + jnp.asarray(neutral, value.dtype)

    def step(position, running):
        longer = join(running, pieces[position])
        return jnp.where(position < mine, longer, running)

    return lax.fori_loop(0, count - 1, step, running)


def add_states(earlier, later):
    return earlier + later


def per_device(queries, keys, values, out_weight):
    tok_rows = queries.shape[0]
    local_heads = queries.shape[1] // HD
    blocks_count = tok_rows // BLOCK
    block_shape = (blocks_count, BLOCK, local_heads, HD)
    query_blocks = queries.reshape(block_shape)
    key_blocks = keys.reshape(block_shape)
    value_blocks = values.reshape(block_shape)
    block_states = jnp.einsum(
        "cthd,cthe->chde", key_blocks, value_blocks, preferred_element_type=jnp.float32
    )
    own_state = jnp.sum(block_states, 0)
    prefix = prefix_2(own_state, "seq", add_states, jnp.zeros_like(own_state))
    earlier = prefix[None] + jnp.cumsum(block_states, 0) - block_states
    causal = jnp.arange(BLOCK)[:, None] >= jnp.arange(BLOCK)[None, :]

    def one_block(inputs):
        query_rows, key_rows, value_rows, carried = inputs
        scores = jnp.einsum(
            "thd,shd->hts", query_rows, key_rows, preferred_element_type=jnp.float32
        )
        scores = jnp.where(causal[None], scores, 0.0).astype(jnp.bfloat16)
        attended = jnp.einsum(
            "hts,shd->thd", scores, value_rows, preferred_element_type=jnp.float32
        )
        attended = attended + jnp.einsum(
            "thd,hde->the",
            query_rows,
            carried.astype(jnp.bfloat16),
            preferred_element_type=jnp.float32,
        )
        normed = attended * lax.rsqrt(jnp.mean(attended * attended, -1, keepdims=True) + 1e-06)
        return normed.astype(jnp.bfloat16).reshape(BLOCK, local_heads * HD)

    mixed_heads = lax.map(one_block, (query_blocks, key_blocks, value_blocks, earlier)).reshape(
        tok_rows, local_heads * HD
    )
    output = jnp.dot(
        lax.all_gather(mixed_heads, "head", axis=1, tiled=True),
        out_weight,
        preferred_element_type=jnp.float32,
    )
    return output.astype(jnp.bfloat16)


def solution(mesh):
    return jax.shard_map(
        per_device,
        mesh=mesh,
        in_specs=(P("seq", "head"), P("seq", "head"), P("seq", "head"), P(None, "head")),
        out_specs=P("seq", "head"),
        check_vma=False,
    )
```

profile of v0, /device:TPU:1, one launch (start us, length us, event | category | flops | bytes accessed | tf_op | source)
XLA Modules:
  0.0 229.1 jit_solution(4268179932716911457)
XLA Ops:
  6.5 1.4 copy.16
  8.0 2.2 fusion.8
  10.6 5.0 %fusion.6 = f32[1024,2,128]{0,2,1:T(8,128)} fusion(pred[1024,1024]{1,0:T(8,128)(4,1)S(1)} %iota_compare_fusion, bf16[1024,2,128]{0,2,1:T(8,128)(2,1)} %bitcast.47, bf16[1024,256]{1,0:T(8,128)(2,1)} %param.8, bf16[1024,256]{1,0:T(8,128)(2,1)} %param.6), kind=kOutput, calls=%fused_computation.9 | convolution fusion | flops 1077936128 | bytes 3670016 | tf_op jit(solution)/shard_map/while/body/eval_jaxpr/hts,shd->thd/dot_general | solution.py:48
  15.6 62.0 %all-gather.6.cloned.1.call-done = f32[64,128,128]{2,1,0:T(8,128)} async-done(((f32[2,128,128]{2,1,0:T(8,128)}), f32[64,128,128]{2,1,0:T(8,128)}) %all-gather.6.cloned.1.call-update) | async-done | bytes 4194320 | tf_op jit(solution)/shard_map/all_gather | solution.py:12
  77.6 30.1 %while.18 = (s32[]{:T(128)}, f32[2,128,128]{2,1,0:T(8,128)S(1)}, s32[]{:T(128)}, f32[32,2,128,128]{3,2,1,0:T(8,128)}, s32[]{:T(128)}, /*index=5*/s32[]{:T(128)}) while((s32[]{:T(128)}, f32[2,128,128]{2,1,0:T(8,128)S(1)}, s32[]{:T(128)}, f32[32,2,128,128]{3,2,1,0:T(8,128)}, s32[]{:T(128)}, /*index=5*/s32[]{:T(128)}) %tuple.42), condition=%wide.region_1.2_spmd.clone, body=%wide.region_0.0_spmd.clone.sunk | while | flops 98308 | bytes 393317 | solution.py:19
  78.6 0.9 add_select_fusion.2
  79.6 0.9 add_select_fusion.2
  80.5 0.9 add_select_fusion.2
  81.5 0.9 add_select_fusion.2
  82.5 0.9 add_select_fusion.2
  83.5 0.9 add_select_fusion.2
  84.4 0.9 add_select_fusion.2
  85.4 0.9 add_select_fusion.2
  86.4 0.9 add_select_fusion.2
  87.4 0.9 add_select_fusion.2
  88.3 0.9 add_select_fusion.2
  89.3 0.9 add_select_fusion.2
  90.3 0.9 add_select_fusion.2
  91.3 0.9 add_select_fusion.2
  92.2 0.9 add_select_fusion.2
  93.2 0.9 add_select_fusion.2
  94.2 0.9 add_select_fusion.2
  95.1 0.9 add_select_fusion.2
  96.1 0.9 add_select_fusion.2
  97.1 0.9 add_select_fusion.2
  98.1 0.9 add_select_fusion.2
  99.0 0.9 add_select_fusion.2
  100.0 0.9 add_select_fusion.2
  101.0 0.9 add_select_fusion.2
  107.8 1.7 multiply_reduce_fusion
  110.5 105.2 %all-gather.4.cloned.1.call-done = bf16[1024,4096]{0,1:T(8,128)(2,1)} async-done(((bf16[1024,256]{0,1:T(8,128)(2,1)}), bf16[1024,4096]{0,1:T(8,128)(2,1)}) %all-gather.4.cloned.1.call-update) | async-done | bytes 8388624 | tf_op jit(solution)/shard_map/all_gather | solution.py:64
  215.7 6.6 %convolution_convert_fusion = bf16[1024,256]{1,0:T(8,128)(2,1)} fusion(bf16[1024,4096]{0,1:T(8,128)(2,1)} %all-gather.4.cloned.1.call-done, bf16[4096,256]{1,0:T(8,128)(2,1)S(1)} %copy-done), kind=kOutput, calls=%fused_computation.10 | convolution fusion | flops 2147745792 | bytes 11010048 | tf_op jit(solution)/shard_map/dot_general | solution.py:63
  (21 shorter events, 8.0 us)
Async XLA Ops:
  6.5 209.1 %copy-start = (bf16[4096,256]{1,0:T(8,128)(2,1)S(1)}, bf16[4096,256]{1,0:T(8,128)(2,1)}, u32[]{:S(2)}) copy-start(bf16[4096,256]{1,0:T(8,128)(2,1)} %param.9) | copy-start | bytes 6291460
  6.5 71.1 %all-gather.6.cloned.1.call-start = ((), (), s32[]{:S(2)}) async-start(), calls=%async_computation.1 | async-start | bytes 4325376 | tf_op jit(solution)/shard_map/all_gather | solution.py:12
  7.9 2.3 copy-start.2
  10.2 205.5 %all-gather.4.cloned.1.call-start = ((), (), s32[]{:S(2)}) async-start(), calls=%async_computation | async-start | bytes 8912896 | tf_op jit(solution)/shard_map/all_gather | solution.py:64
  10.6 97.2 %copy-start.1 = (f32[2,128,128]{2,1,0:T(8,128)S(1)}, f32[2,128,128]{2,1,0:T(8,128)}, u32[]{:S(2)}) copy-start(f32[2,128,128]{2,1,0:T(8,128)} %fusion.8) | copy-start | bytes 393220
Sparse Core Ops, SparseCore 0:
  10.5 67.0 all-gather.5
  110.6 105.0 all-gather.3
where the time goes:
time: 230 us; the launch traced here: 229 us
  waiting for transfers between devices  167 us (73%)
  other arithmetic  30.7 us (13%)
  matrix products  15.6 us (7%)
  between operations  13.5 us (6%)
    all_gather x1, waiting for transfers between devices, per_device(): lax.all_gather(mixed_heads, 'head', axis=1, tiled=True)  105 us
    all_gather x1, waiting for transfers between devices, prefix_2(): pieces = lax.all_gather(value, axis)  62 us
    select_n x31, other arithmetic, step(): return jnp.where(position < mine, longer, running)  29.4 us
    dot_general x1, matrix products, per_device(): jnp.dot(lax.all_gather(mixed_heads, 'head', axis=1, tiled=True), out_weig...  6.55 us
    dot_general x1, matrix products, one_block(): jnp.einsum('hts,shd->thd', scores, value_rows, preferred_element_type=jnp...  5.05 us
  transfers between devices with their start and end apart: 2, of which 2 were waited for; matrix products, arithmetic and copies ran while one was open for 2% of the time, Pallas kernels for 0%

commit v1 on v0

--- a/solution.py
+++ b/solution.py
@@ -60,10 +60,11 @@
     mixed_heads = lax.map(one_block, (query_blocks, key_blocks, value_blocks, earlier)).reshape(
         tok_rows, local_heads * HD
     )
+    edit_steps_all = lambda xs, ndim_at: jnp.concatenate(
+        lax.all_to_all(jnp.stack(lax.axis_size("head") * [xs]), "head", 0, 0), axis=ndim_at
+    )
     output = jnp.dot(
-        lax.all_gather(mixed_heads, "head", axis=1, tiled=True),
-        out_weight,
-        preferred_element_type=jnp.float32,
+        edit_steps_all(mixed_heads, ndim_at=1), out_weight, preferred_element_type=jnp.float32
     )
     return output.astype(jnp.bfloat16)
 

time: 230 us -> 499 us (2.17); the launches traced: 229 us -> 492 us
  blocking collectives: 0 us -> 372 us
  waiting for transfers between devices: 167 us -> 62.1 us
    all_to_all x0 -> x1, blocking collectives: none -> 372 us  [per_device(): lax.all_to_all(jnp.stack(lax.axis_size('head') * [xs]), 'head', 0, 0)]
    all_gather x1 -> x0, waiting for transfers between devices: 105 us -> none  [per_device(): lax.all_gather(mixed_heads, 'head', axis=1, tiled=True)]
  transfers between devices with their start and end apart: 2 -> 1, of which waited for: 2 -> 1; matrix products, arithmetic and copies ran while one was open for 2% -> 1% of each run, Pallas kernels for 0% -> 0%
where the time goes in v1:
time: 499 us; the launch traced here: 492 us
  blocking collectives  372 us (75%)
  waiting for transfers between devices  62.1 us (12%)
  other arithmetic  29.9 us (6%)
  between operations  13.5 us (3%)
  matrix products  12.2 us (2%)
    all_to_all x1, blocking collectives, per_device(): lax.all_to_all(jnp.stack(lax.axis_size('head') * [xs]), 'head', 0, 0)  372 us
    all_gather x1, waiting for transfers between devices, prefix_2(): pieces = lax.all_gather(value, axis)  62.1 us
    select_n x31, other arithmetic, step(): return jnp.where(position < mine, longer, running)  29.4 us
  transfers between devices with their start and end apart: 1, of which 1 were waited for; matrix products, arithmetic and copies ran while one was open for 1% of the time, Pallas kernels for 0%

profile of v1, /device:TPU:1, one launch (start us, length us, event | category | flops | bytes accessed | tf_op | source)
XLA Modules:
  0.0 492.3 jit_solution(12565084924182406021)
XLA Ops:
  6.5 1.4 copy.24
  8.0 2.2 fusion.8
  10.5 5.1 %fusion.6 = f32[1024,2,128]{0,2,1:T(8,128)} fusion(pred[1024,1024]{1,0:T(8,128)(4,1)S(1)} %iota_compare_fusion, bf16[1024,2,128]{0,2,1:T(8,128)(2,1)} %bitcast.51, bf16[1024,256]{1,0:T(8,128)(2,1)} %param.8, bf16[1024,256]{1,0:T(8,128)(2,1)} %param.6), kind=kOutput, calls=%fused_computation.9 | convolution fusion | flops 1077936128 | bytes 3670016 | tf_op jit(solution)/shard_map/while/body/eval_jaxpr/hts,shd->thd/dot_general | solution.py:48
  15.6 62.1 %all-gather.3.cloned.1.call-done = f32[64,128,128]{2,1,0:T(8,128)} async-done(((f32[2,128,128]{2,1,0:T(8,128)}), f32[64,128,128]{2,1,0:T(8,128)}) %all-gather.3.cloned.1.call-update) | async-done | bytes 4194320 | tf_op jit(solution)/shard_map/all_gather | solution.py:12
  77.6 30.1 %while.18 = (s32[]{:T(128)}, f32[2,128,128]{2,1,0:T(8,128)S(1)}, s32[]{:T(128)}, f32[32,2,128,128]{3,2,1,0:T(8,128)}, s32[]{:T(128)}, /*index=5*/s32[]{:T(128)}) while((s32[]{:T(128)}, f32[2,128,128]{2,1,0:T(8,128)S(1)}, s32[]{:T(128)}, f32[32,2,128,128]{3,2,1,0:T(8,128)}, s32[]{:T(128)}, /*index=5*/s32[]{:T(128)}) %tuple.40), condition=%wide.region_1.2_spmd.clone, body=%wide.region_0.0_spmd.clone.sunk | while | flops 98308 | bytes 393317 | solution.py:19
  78.6 0.9 add_select_fusion.2
  79.6 0.9 add_select_fusion.2
  80.5 0.9 add_select_fusion.2
  81.5 0.9 add_select_fusion.2
  82.5 0.9 add_select_fusion.2
  83.5 0.9 add_select_fusion.2
  84.4 0.9 add_select_fusion.2
  85.4 0.9 add_select_fusion.2
  86.4 0.9 add_select_fusion.2
  87.4 0.9 add_select_fusion.2
  88.3 0.9 add_select_fusion.2
  89.3 0.9 add_select_fusion.2
  90.3 0.9 add_select_fusion.2
  91.3 0.9 add_select_fusion.2
  92.2 0.9 add_select_fusion.2
  93.2 0.9 add_select_fusion.2
  94.2 0.9 add_select_fusion.2
  95.1 0.9 add_select_fusion.2
  96.1 0.9 add_select_fusion.2
  97.1 0.9 add_select_fusion.2
  98.1 0.9 add_select_fusion.2
  99.0 0.9 add_select_fusion.2
  100.0 0.9 add_select_fusion.2
  107.8 1.7 multiply_reduce_fusion
  109.7 1.1 stack.3
  110.7 371.5 %all_to_all.5 = bf16[16,1024,256]{1,2,0:T(8,128)(2,1)S(1)} all-to-all(bf16[16,1024,256]{1,2,0:T(8,128)(2,1)S(1)} %stack.3), channel_id=1, replica_groups=mesh['seq'=32,'head'=16] {'head'}, dimensions={0} | all-to-all | bytes 16777216 | tf_op jit(solution)/shard_map/all_to_all | solution.py:64
  482.3 3.2 convolution_convert_fusion
  (20 shorter events, 8.1 us)
Async XLA Ops:
  6.5 475.7 %copy-start = (bf16[4096,256]{1,0:T(8,128)(2,1)S(1)}, bf16[4096,256]{1,0:T(8,128)(2,1)}, u32[]{:S(2)}) copy-start(bf16[4096,256]{1,0:T(8,128)(2,1)} %param.9) | copy-start | bytes 6291460
  6.5 71.1 %all-gather.3.cloned.1.call-start = ((), (), s32[]{:S(2)}) async-start(), calls=%async_computation.1 | async-start | bytes 4325376 | tf_op jit(solution)/shard_map/all_gather | solution.py:12
  7.9 2.2 copy-start.2
  10.5 97.3 %copy-start.1 = (f32[2,128,128]{2,1,0:T(8,128)S(1)}, f32[2,128,128]{2,1,0:T(8,128)}, u32[]{:S(2)}) copy-start(f32[2,128,128]{2,1,0:T(8,128)} %fusion.8) | copy-start | bytes 393220
Sparse Core Ops, SparseCore 0:
  10.5 67.0 all-gather.2
